TPU v7x, 32 devices: a whole 2x2x4 slice. The times are simulated.
32 devices in a mesh: cube: 4 (over z), front: 8 (over y, x, core).
Axes of the slice: x: 2, y: 2, z: 4, core: 2. Of those that a mesh axis runs over, the one named last changes fastest.
Arguments:
- right_sides: float32 [3, 4, 512, 128], P(None, 'cube', 'front'), may hold values from -6 to 6
- inverse_leaf: float32 [4, 512, 512], P('cube', 'front'), may hold values from -2 to 2, as said below
- inverse_mid: float32 [4, 512, 1024], P('cube', 'front'), may hold values from -2 to 2, as said below
- inverse_top: float32 [4, 512, 2048], P('cube', 'front'), may hold values from -2 to 2, as said below
- coupling_mid: float32 [4, 512, 1024], P('cube', 'front'), may hold values from -0.25 to 0.25
- coupling_top: float32 [4, 512, 2048], P('cube', 'front'), may hold values from -0.1875 to 0.1875
- pattern_mid: int32 [4, 8, 16], P('cube', 'front'), may hold values 0 or 1
- pattern_top: int32 [4, 8, 32], P('cube', 'front'), may hold values 0 or 1
Outputs:
- solution: float32 [3, 4, 512, 128], P(None, 'cube', 'front')
Inputs may be any that keep to these rules, and one draw needn't show every extreme that they name: `inverse_leaf`: each block is the inverse of a lower triangular diagonal block: zero above the diagonal of the separator's row order, diagonal 1 to 2. `inverse_mid`: as inverse_leaf. `inverse_top`: as inverse_leaf.
All inputs are finite; a program needn't handle non-finite values. No bound on the sum of `pattern_mid` or of `pattern_top` on one device may be relied on, other than what follows from the above.
Results may differ from a plain program's by a relative error of at most 0.00013.
Values sent between devices are 32-bit elements; how exact they have to be, the bound alone decides.
No kernel may reach another device: no remote copies, remote signals or barrier semaphores. Data moves between devices by JAX's collectives and lax.ppermute only.
A program may use at most 64 MiB of HBM per device.

v0:
```python
import jax
import jax.numpy as jnp
from jax import lax
from jax.sharding import PartitionSpec as P

TILE = 64


def from_partner(value, axis, distance):
    mask = 2**distance
    pairs = [(source, source ^ mask) for source in range(lax.axis_size(axis))]
    return lax.ppermute(value, axis, pairs)


def masked(coupling, pattern):
    keep_rows = jnp.repeat(pattern[0], TILE, axis=0)
    keep_all = jnp.repeat(keep_rows, TILE, axis=1)
    return coupling[0] * keep_all.astype(jnp.float32)


def members_of(local_rows, count, cube_pos):
    if count == 1:
        return local_rows[None]
    stacked = local_rows[None]
    for bit_index in range(count.bit_length() - 1):
        partner = from_partner(stacked, "cube", bit_index)
        upper = cube_pos // 2**bit_index % 2
        stacked = jnp.where(
            upper == 0,
            jnp.concatenate([stacked, partner], 0),
            jnp.concatenate([partner, stacked], 0),
        )
    return stacked


def gathered_product(matrix, stacked):
    count = stacked.shape[0]
    height = matrix.shape[0]
    member_width = matrix.shape[1] // count
    shaped = matrix.reshape(height, count, member_width)
    return jnp.einsum(
        "rms,msn->rn",
        shaped,
        lax.all_gather(stacked, "front", axis=1, tiled=True),
        precision=lax.Precision.HIGHEST,
        preferred_element_type=jnp.float32,
    )


def spread_back(matrix, local_rows, count, cube_pos):
    height = matrix.shape[0]
    member_width = matrix.shape[1] // count
    shaped = matrix.reshape(height, count, member_width)
    summed = lax.psum_scatter(
        jnp.einsum(
            "rms,rn->smn",
            shaped,
            local_rows,
            precision=lax.Precision.HIGHEST,
            preferred_element_type=jnp.float32,
        ),
        "front",
        scatter_dimension=0,
        tiled=True,
    )
    if count == 1:
        return summed[:, 0]
    stacked = summed
    for bit_index in reversed(range(count.bit_length() - 1)):
        half_size = stacked.shape[1] // 2
        upper = cube_pos // 2**bit_index % 2
        kept = lax.dynamic_slice_in_dim(stacked, upper * half_size, half_size, 1)
        outgoing = lax.dynamic_slice_in_dim(stacked, (1 - upper) * half_size, half_size, 1)
        stacked = kept + from_partner(outgoing, "cube", bit_index)
    return stacked[:, 0]


def local(
    right_sides,
    inverse_leaf,
    inverse_mid,
    inverse_top,
    coupling_mid,
    coupling_top,
    pattern_mid,
    pattern_top,
):
    cube_pos = lax.axis_index("cube")
    block_mid = masked(coupling_mid, pattern_mid)
    block_top = masked(coupling_top, pattern_top)
    inv_leaf = inverse_leaf[0]
    inv_mid = inverse_mid[0]
    inv_top = inverse_top[0]
    sides = right_sides[:, 0]
    solved_leaf = gathered_product(inv_leaf, members_of(sides[0], 1, cube_pos))
    update_mid = gathered_product(block_mid, members_of(solved_leaf, 2, cube_pos))
    solved_mid = gathered_product(inv_mid, members_of(sides[1] - update_mid, 2, cube_pos))
    update_top = gathered_product(block_top, members_of(solved_mid, 4, cube_pos))
    solved_top = gathered_product(inv_top, members_of(sides[2] - update_top, 4, cube_pos))
    back_top = spread_back(inv_top, solved_top, 4, cube_pos)
    carry_mid = spread_back(block_top, back_top, 4, cube_pos)
    back_mid = spread_back(inv_mid, solved_mid - carry_mid, 2, cube_pos)
    carry_leaf = spread_back(block_mid, back_mid, 2, cube_pos)
    back_leaf = spread_back(inv_leaf, solved_leaf - carry_leaf, 1, cube_pos)
    result = jnp.stack([back_leaf, back_mid, back_top])
    return result[:, None]


def solution(mesh):
    return jax.shard_map(
        local,
        mesh=mesh,
        in_specs=(
            P(None, "cube", "front", None),
            P("cube", "front", None),
            P("cube", "front", None),
            P("cube", "front", None),
            P("cube", "front", None),
            P("cube", "front", None),
            P("cube", "front", None),
            P("cube", "front", None),
        ),
        out_specs=P(None, "cube", "front", None),
        check_vma=False,
    )
```

profile of v0, /device:TPU:0, one launch (start us, length us, event | category | flops | bytes accessed | tf_op | source)
XLA Modules:
  0.0 384.1 jit_solution(2500228545821510919)
XLA Ops:
  7.4 10.8 %all-gather = f32[1,1,512,128]{3,2,1,0:T(8,128)S(1)} all-gather(f32[1,1,64,128]{3,2,1,0:T(8,128)S(1)} %slice-done), channel_id=2, replica_groups=mesh['cube'=4,'front'=8] {'front'}, dimensions={2}, use_global_device_ids=true | all-gather | bytes 294912 | tf_op jit(solution)/shard_map/all_gather | solution.py:44
  18.4 1.6 collective-permute-start
  20.6 1.8 collective-permute-done
  22.4 10.0 %all_gather.16 = f32[2,512,128]{2,1,0:T(8,128)S(1)} all-gather(f32[2,64,128]{2,1,0:T(8,128)S(1)} %maximum_select_fusion.2), channel_id=1, replica_groups=mesh['cube'=4,'front'=8] {'front'}, dimensions={1}, use_global_device_ids=true | all-gather | bytes 589824 | tf_op jit(solution)/shard_map/all_gather | solution.py:44
  32.9 1.6 collective-permute-start.1
  34.7 2.1 collective-permute-done.1
  36.8 8.9 %all_gather.17 = f32[2,512,128]{2,1,0:T(8,128)S(1)} all-gather(f32[2,64,128]{2,1,0:T(8,128)S(1)} %maximum_select_fusion.3), channel_id=1, replica_groups=mesh['cube'=4,'front'=8] {'front'}, dimensions={1}, use_global_device_ids=true | all-gather | bytes 589824 | tf_op jit(solution)/shard_map/all_gather | solution.py:44
  46.2 1.6 collective-permute-start.2
  47.8 2.3 collective-permute-done.2
  50.2 2.7 collective-permute-start.3
  52.8 2.6 collective-permute-done.3
  57.0 23.5 %all-gather.4.cloned.1.call-done = f32[4,512,128]{2,1,0:T(8,128)} async-done(((f32[4,64,128]{2,1,0:T(8,128)}), f32[4,512,128]{2,1,0:T(8,128)}) %all-gather.4.cloned.1.call-update) | async-done | bytes 1048592 | tf_op jit(solution)/shard_map/all_gather | solution.py:44
  80.5 2.1 fusion.1
  82.6 1.6 collective-permute-start.4
  84.1 2.4 collective-permute-done.4
  86.6 2.5 collective-permute-start.5
  89.0 2.8 collective-permute-done.5
  92.9 23.8 %all-gather.6.cloned.1.call-done = f32[4,512,128]{2,1,0:T(8,128)} async-done(((f32[4,64,128]{2,1,0:T(8,128)}), f32[4,512,128]{2,1,0:T(8,128)}) %all-gather.6.cloned.1.call-update) | async-done | bytes 1048592 | tf_op jit(solution)/shard_map/all_gather | solution.py:44
  116.7 2.1 fusion.5
  118.8 1.1 convolution_bitcast_fusion.1
  119.8 1.3 copy.25
  123.1 54.9 %all-reduce.5.cloned.1.call-done = f32[512,4,128]{2,1,0:T(4,128)} async-done(((f32[512,4,128]{2,1,0:T(4,128)}), f32[512,4,128]{2,1,0:T(4,128)}) %all-reduce.5.cloned.1.call-update) | async-done | bytes 1048592
  178.0 0.9 constant_dynamic-slice_fusion.6
  179.0 2.4 collective-permute-start.6
  181.5 2.7 collective-permute-done.6
  184.2 0.9 dynamic-slice_add_fusion
  185.2 1.5 collective-permute-start.7
  187.1 2.1 collective-permute-done.7
  189.2 2.8 convolution_bitcast_fusion
  192.3 35.8 %reduce-scatter.4.cloned.1.call-done = f32[64,4,128]{2,0,1:T(8,128)} async-done(((f32[512,4,128]{2,0,1:T(8,128)}), f32[64,4,128]{2,0,1:T(8,128)}) %reduce-scatter.4.cloned.1.call-update) | async-done | bytes 131088 | tf_op jit(solution)/shard_map/reduce_scatter | solution.py:54
  228.2 0.9 constant_dynamic-slice_fusion.4
  229.1 2.4 collective-permute-start.8
  231.5 2.9 collective-permute-done.8
  234.4 1.4 collective-permute-start.9
  235.8 2.6 collective-permute-done.9
  239.0 1.0 copy.29
  240.3 55.3 %all-reduce.7.cloned.1.call-done = f32[512,2,128]{2,1,0:T(2,128)} async-done(((f32[512,2,128]{2,1,0:T(2,128)}), f32[512,2,128]{2,1,0:T(2,128)}) %all-reduce.7.cloned.1.call-update) | async-done | bytes 524304
  295.6 1.0 constant_dynamic-slice_fusion.2
  296.6 1.5 collective-permute-start.10
  298.3 2.3 collective-permute-done.10
  300.5 1.8 convolution_bitcast_fusion.2
  302.4 33.5 %reduce-scatter.6.cloned.1.call-done = f32[64,2,128]{2,0,1:T(8,128)} async-done(((f32[512,2,128]{2,0,1:T(8,128)}), f32[64,2,128]{2,0,1:T(8,128)}) %reduce-scatter.6.cloned.1.call-update) | async-done | bytes 65552 | tf_op jit(solution)/shard_map/reduce_scatter | solution.py:54
  336.0 0.8 constant_dynamic-slice_fusion.1
  336.8 1.5 collective-permute-start.11
  338.3 2.4 collective-permute-done.11
  341.1 0.8 copy.34
  342.0 33.8 %reduce-scatter.8.cloned.1.call-done = f32[64,1,128]{2,1,0:T(1,128)} async-done(((f32[512,1,128]{2,1,0:T(1,128)}), f32[64,1,128]{2,1,0:T(1,128)}) %reduce-scatter.8.cloned.1.call-update) | async-done | bytes 32784 | tf_op jit(solution)/shard_map/reduce_scatter | solution.py:54
  375.8 1.4 maximum_bitcast_fusion
  (77 shorter events, 9.1 us)
Async XLA Ops:
  6.5 11.6 %copy-start = (f32[1,64,512]{2,1,0:T(8,128)S(1)}, f32[1,64,512]{2,1,0:T(8,128)}, u32[]{:S(2)}) copy-start(f32[1,64,512]{2,1,0:T(8,128)} %param.9) | copy-start | bytes 393220
  6.5 0.8 slice-start
  6.5 73.9 %all-gather.4.cloned.1.call-start = ((), (), s32[]{:S(2)}) async-start(), calls=%async_computation.3 | async-start | bytes 1179648 | tf_op jit(solution)/shard_map/all_gather | solution.py:44
  18.1 2.0 copy-start.2
  18.4 1.7 copy-start.9
  18.4 4.0 %collective-permute-start = (f32[1,64,128]{2,1,0:T(8,128)S(1)}, f32[1,64,128]{2,1,0:T(8,128)S(1)}, u32[]{:S(2)}, u32[]{:S(2)}) collective-permute-start(f32[1,64,128]{2,1,0:T(8,128)S(1)} %bitcast.93), channel_id=1, source_target_pairs={{0,8},{8,0},{16,24},{24,16},{1,9},{9,1},{17,25},{25,17},{2,10},{10... | collective-permute-start | bytes 98312 | tf_op jit(solution)/shard_map/ppermute | solution.py:12
  22.4 10.0 %copy-start.6 = (f32[3,1,64,128]{3,2,1,0:T(8,128)S(1)}, f32[3,1,64,128]{3,2,1,0:T(8,128)}, u32[]{:S(2)}) copy-start(f32[3,1,64,128]{3,2,1,0:T(8,128)} %param.8) | copy-start | bytes 294916
  32.4 2.1 copy-start.4
  32.9 4.0 %collective-permute-start.1 = (f32[1,64,128]{2,1,0:T(8,128)S(1)}, f32[1,64,128]{2,1,0:T(8,128)S(1)}, u32[]{:S(2)}, u32[]{:S(2)}) collective-permute-start(f32[1,64,128]{2,1,0:T(8,128)S(1)} %fusion.3), channel_id=1, source_target_pairs={{0,8},{8,0},{16,24},{24,16},{1,9},{9,1},{17,25},{25,17},{2,10},{10... | collective-permute-start | bytes 98312 | tf_op jit(solution)/shard_map/ppermute | solution.py:12
  45.7 10.4 %copy-start.1 = (f32[1,64,2048]{2,1,0:T(8,128)S(1)}, f32[1,64,2048]{2,1,0:T(8,128)}, u32[]{:S(2)}) copy-start(f32[1,64,2048]{2,1,0:T(8,128)} %param.13) | copy-start | bytes 1572868
  46.2 4.0 %collective-permute-start.2 = (f32[1,64,128]{2,1,0:T(8,128)S(1)}, f32[1,64,128]{2,1,0:T(8,128)S(1)}, u32[]{:S(2)}, u32[]{:S(2)}) collective-permute-start(f32[1,64,128]{2,1,0:T(8,128)S(1)} %bitcast.89), channel_id=1, source_target_pairs={{0,8},{8,0},{16,24},{24,16},{1,9},{9,1},{17,25},{25,17},{2,10},{10... | collective-permute-start | bytes 98312 | tf_op jit(solution)/shard_map/ppermute | solution.py:12
  50.2 5.2 %collective-permute-start.3 = (f32[2,64,128]{2,1,0:T(8,128)S(1)}, f32[2,64,128]{2,1,0:T(8,128)S(1)}, u32[]{:S(2)}, u32[]{:S(2)}) collective-permute-start(f32[2,64,128]{2,1,0:T(8,128)S(1)} %maximum_select_fusion.4), channel_id=1, source_target_pairs={{0,16},{8,24},{16,0},{24,8},{1,17},{9,25},{17,1},{25,9},{2,18},{10... | collective-permute-start | bytes 196616 | tf_op jit(solution)/shard_map/ppermute | solution.py:12
  56.1 0.7 copy-start.8
  56.1 60.6 %all-gather.6.cloned.1.call-start = ((), (), s32[]{:S(2)}) async-start(), calls=%async_computation.4 | async-start | bytes 1179648 | tf_op jit(solution)/shard_map/all_gather | solution.py:44
  82.5 10.0 %copy-start.3 = (f32[1,64,2048]{2,1,0:T(8,128)S(1)}, f32[1,64,2048]{2,1,0:T(8,128)}, u32[]{:S(2)}) copy-start(f32[1,64,2048]{2,1,0:T(8,128)} %param.11) | copy-start | bytes 1572868
  82.6 4.0 %collective-permute-start.4 = (f32[1,64,128]{2,1,0:T(8,128)S(1)}, f32[1,64,128]{2,1,0:T(8,128)S(1)}, u32[]{:S(2)}, u32[]{:S(2)}) collective-permute-start(f32[1,64,128]{2,1,0:T(8,128)S(1)} %fusion.1), channel_id=1, source_target_pairs={{0,8},{8,0},{16,24},{24,16},{1,9},{9,1},{17,25},{25,17},{2,10},{10... | collective-permute-start | bytes 98312 | tf_op jit(solution)/shard_map/ppermute | solution.py:12
  86.6 5.2 %collective-permute-start.5 = (f32[2,64,128]{2,1,0:T(8,128)S(1)}, f32[2,64,128]{2,1,0:T(8,128)S(1)}, u32[]{:S(2)}, u32[]{:S(2)}) collective-permute-start(f32[2,64,128]{2,1,0:T(8,128)S(1)} %maximum_select_fusion.5), channel_id=1, source_target_pairs={{0,16},{8,24},{16,0},{24,8},{1,17},{9,25},{17,1},{25,9},{2,18},{10... | collective-permute-start | bytes 196616 | tf_op jit(solution)/shard_map/ppermute | solution.py:12
  92.5 85.6 %all-reduce.5.cloned.1.call-start = ((), (), s32[]{:S(2)}) async-start(), calls=%async_computation.8 | async-start | bytes 2097152
  121.2 107.0 %reduce-scatter.4.cloned.1.call-start = ((), (), s32[]{:S(2)}) async-start(), calls=%async_computation.5 | async-start | bytes 1179648 | tf_op jit(solution)/shard_map/reduce_scatter | solution.py:54
  121.2 0.7 copy-start.10
  179.0 5.2 %collective-permute-start.6 = (f32[64,2,128]{2,1,0:T(2,128)S(1)}, f32[64,2,128]{2,1,0:T(2,128)S(1)}, u32[]{:S(2)}, u32[]{:S(2)}) collective-permute-start(f32[64,2,128]{2,1,0:T(2,128)S(1)} %constant_dynamic-slice_fusion.6), channel_id=1, source_target_pairs={{0,16},{8,24},{16,0},{24,8},{1,17},{9,25},{17,1},{25,9},{2,18},{10... | collective-permute-start | bytes 196616 | tf_op jit(solution)/shard_map/ppermute | solution.py:12
  185.2 4.0 %collective-permute-start.7 = (f32[64,1,128]{2,1,0:T(1,128)S(1)}, f32[64,1,128]{2,1,0:T(1,128)S(1)}, u32[]{:S(2)}, u32[]{:S(2)}) collective-permute-start(f32[64,1,128]{2,1,0:T(1,128)S(1)} %constant_dynamic-slice_fusion.5), channel_id=1, source_target_pairs={{0,8},{8,0},{16,24},{24,16},{1,9},{9,1},{17,25},{25,17},{2,10},{10... | collective-permute-start | bytes 98312 | tf_op jit(solution)/shard_map/ppermute | solution.py:12
  192.1 103.5 %all-reduce.7.cloned.1.call-start = ((), (), s32[]{:S(2)}) async-start(), calls=%async_computation.9 | async-start | bytes 1048576
  228.2 6.2 %copy-start.5 = (f32[64,4,128]{2,0,1:T(8,128)S(1)}, f32[64,4,128]{2,0,1:T(8,128)}, u32[]{:S(2)}) copy-start(f32[64,4,128]{2,0,1:T(8,128)} %reduce-scatter.4.cloned.1.call-done) | copy-start | bytes 393220
  229.1 5.3 %collective-permute-start.8 = (f32[64,2,128]{2,0,1:T(8,128)S(1)}, f32[64,2,128]{2,0,1:T(8,128)S(1)}, u32[]{:S(2)}, u32[]{:S(2)}) collective-permute-start(f32[64,2,128]{2,0,1:T(8,128)S(1)} %constant_dynamic-slice_fusion.4), channel_id=1, source_target_pairs={{0,16},{8,24},{16,0},{24,8},{1,17},{9,25},{17,1},{25,9},{2,18},{10... | collective-permute-start | bytes 196616 | tf_op jit(solution)/shard_map/ppermute | solution.py:12
  234.4 4.0 %collective-permute-start.9 = (f32[64,1,128]{2,0,1:T(8,128)S(1)}, f32[64,1,128]{2,0,1:T(8,128)S(1)}, u32[]{:S(2)}, u32[]{:S(2)}) collective-permute-start(f32[64,1,128]{2,0,1:T(8,128)S(1)} %constant_dynamic-slice_fusion.3), channel_id=1, source_target_pairs={{0,8},{8,0},{16,24},{24,16},{1,9},{9,1},{17,25},{25,17},{2,10},{10... | collective-permute-start | bytes 98312 | tf_op jit(solution)/shard_map/ppermute | solution.py:12
  240.0 95.9 %reduce-scatter.6.cloned.1.call-start = ((), (), s32[]{:S(2)}) async-start(), calls=%async_computation.6 | async-start | bytes 589824 | tf_op jit(solution)/shard_map/reduce_scatter | solution.py:54
  296.6 4.0 %collective-permute-start.10 = (f32[64,1,128]{2,0,1:T(8,128)S(1)}, f32[64,1,128]{2,0,1:T(8,128)S(1)}, u32[]{:S(2)}, u32[]{:S(2)}) collective-permute-start(f32[64,1,128]{2,0,1:T(8,128)S(1)} %bitcast.97), channel_id=1, source_target_pairs={{0,8},{8,0},{16,24},{24,16},{1,9},{9,1},{17,25},{25,17},{2,10},{10... | collective-permute-start | bytes 98312 | tf_op jit(solution)/shard_map/ppermute | solution.py:12
  302.4 73.5 %reduce-scatter.8.cloned.1.call-start = ((), (), s32[]{:S(2)}) async-start(), calls=%async_computation.7 | async-start | bytes 294912 | tf_op jit(solution)/shard_map/reduce_scatter | solution.py:54
  335.9 4.8 %copy-start.7 = (f32[64,2,128]{2,0,1:T(8,128)S(1)}, f32[64,2,128]{2,0,1:T(8,128)}, u32[]{:S(2)}) copy-start(f32[64,2,128]{2,0,1:T(8,128)} %reduce-scatter.6.cloned.1.call-done) | copy-start | bytes 196612
  336.8 3.9 %collective-permute-start.11 = (f32[64,1,128]{2,0,1:T(8,128)S(1)}, f32[64,1,128]{2,0,1:T(8,128)S(1)}, u32[]{:S(2)}, u32[]{:S(2)}) collective-permute-start(f32[64,1,128]{2,0,1:T(8,128)S(1)} %constant_dynamic-slice_fusion.1), channel_id=1, source_target_pairs={{0,8},{8,0},{16,24},{24,16},{1,9},{9,1},{17,25},{25,17},{2,10},{10... | collective-permute-start | bytes 98312 | tf_op jit(solution)/shard_map/ppermute | solution.py:12
Sparse Core Ops, SparseCore 0:
  56.2 24.2 all-gather.3
  92.6 24.0 all-gather.5
  121.3 56.7 all-reduce.4
  192.2 35.9 reduce-scatter.3
  240.2 55.3 all-reduce.6
  302.5 33.4 reduce-scatter.5
  342.1 33.6 reduce-scatter.7
where the time goes:
time: 385 us; the launch traced here: 384 us
  waiting for transfers between devices  290 us (75%)
  blocking collectives  29.6 us (8%)
  starting transfers between devices  22.7 us (6%)
  between operations  14.4 us (4%)
  matrix products  12.1 us (3%)
  local copies, waits for them, and re-layouts  11.6 us (3%)
  other arithmetic  3.85 us (1%)
    unnamed x9, waiting for transfers between devices  110 us
    reduce_scatter x3, waiting for transfers between devices, spread_back(): lax.psum_scatter(jnp.einsum('rms,rn->smn', shaped, local_rows, precision=...  103 us
    all_gather x2, waiting for transfers between devices, gathered_product(): lax.all_gather(stacked, 'front', axis=1, tiled=True)  47.3 us
    all_gather x3, blocking collectives, gathered_product(): lax.all_gather(stacked, 'front', axis=1, tiled=True)  29.6 us
    ppermute x12, waiting for transfers between devices, from_partner(): return lax.ppermute(value, axis, pairs)  28.9 us
    ppermute x12, starting transfers between devices, from_partner(): return lax.ppermute(value, axis, pairs)  22.3 us
  transfers between devices with their start and end apart: 19, of which 19 were waited for; matrix products, arithmetic and copies ran while one was open for 1% of the time, Pallas kernels for 0%

commit v1 on v0

v1 whole, which is shorter than its diff:
```python
import functools

import jax
import jax.numpy as jnp
from jax import lax
from jax.experimental import pallas as pl
from jax.experimental.pallas import tpu as pltpu
from jax.sharding import PartitionSpec as P

TILE = 64
TEAM = 4
F32, BF16 = jnp.float32, jnp.bfloat16


def exchange(value, axis, mask):
    pairs = [(source, source ^ mask) for source in range(lax.axis_size(axis))]
    return lax.ppermute(value, axis, pairs)


def call(kernel, outs, *operands, scratch=()):
    smem = pl.BlockSpec(memory_space=pltpu.SMEM)
    vmem = pl.BlockSpec(memory_space=pltpu.VMEM)
    specs = [smem if value.dtype == jnp.int32 else vmem for value in operands]
    return pl.pallas_call(
        kernel,
        out_shape=[jax.ShapeDtypeStruct(shape, dtype) for shape, dtype in outs],
        in_specs=specs,
        out_specs=[vmem] * len(outs),
        scratch_shapes=list(scratch),
    )(*operands)


def split(value):
    high = value.astype(BF16)
    return high, (value - high.astype(F32)).astype(BF16)


def product(value, high, low, contract):
    dims = (((1,), (contract,)), ((), ()))
    dot = functools.partial(lax.dot_general, dimension_numbers=dims, preferred_element_type=F32)
    first, second = split(value)
    return dot(first, high) + (dot(second, high) + dot(first, low))


def team_order(pieces, g):
    join = lambda a, b: jnp.concatenate([a, b], axis=-1)
    inner = [
        jnp.where(g % 2 == 0, join(pieces[m], pieces[m + 1]), join(pieces[m + 1], pieces[m]))
        for m in (0, 2)
    ]
    return jnp.where(g // 2 == 0, join(*inner), join(inner[1], inner[0]))


def team_pieces(value, g):
    half = value.shape[-1] // 2
    sides = value[..., :half], value[..., half:]
    pieces = []
    for first, second in (sides, sides[::-1]):
        same = jnp.where(g // 2 == 0, first, second)
        parts = same[..., : half // 2], same[..., half // 2 :]
        for a, b in (parts, parts[::-1]):
            pieces.append(jnp.where(g % 2 == 0, a, b))
    return pieces


def slice_columns(matrix, outs, index, blocks):
    parts, width = len(outs), outs[0].shape[1] // blocks
    for m, out in enumerate(outs):
        for block in range(blocks):
            start = pl.multiple_of((block * parts + (index ^ m)) * width, 128)
            out[:, block * width : (block + 1) * width] = matrix[0, :, pl.ds(start, width)]


def slice_masked(matrix, pattern, outs, index):
    _, width = outs[0].shape
    lane = lax.broadcasted_iota(jnp.int32, (1, 128), 1)
    for m, out in enumerate(outs):
        start = (index ^ m) * width
        for block in range(width // 128):
            at = pl.multiple_of(start + block * 128, 128)
            keep = jnp.zeros((1, 128), F32)
            for tile in range(128 // TILE):
                bit = pattern[0, 0, (start + block * 128) // TILE + tile].astype(F32)
                keep = jnp.where(lane // TILE == tile, bit, keep)
            out[:, block * 128 : (block + 1) * 128] = matrix[0, :, pl.ds(at, 128)] * keep


def prepare_leaf(place, matrix, sides, *rest):
    parts = len(rest) - 1 - TEAM
    outs, pieces, turned = rest[:parts], rest[parts:-1], rest[-1]
    g, q = place[0], place[1]
    slice_columns(matrix, outs, q, 1)
    for level in range(sides.shape[0]):
        turned[level] = sides[level, 0].T
    width = turned.shape[1] // TEAM
    for m, piece in enumerate(pieces):
        start = pl.multiple_of((g ^ m) * width, 8)
        piece[...] = turned[:, pl.ds(start, width), :]


def prepare_level(slot, count, place, coupling, pattern, inverse, *outs):
    slice_masked(coupling, pattern, outs[:count], place[slot])
    slice_columns(inverse, outs[count:], place[1], count)


def assemble(slot, rows, place, own, across, beside, both, high, low):
    g, index = place[0], place[slot]
    for m_team, piece in ((0, own), (2, across), (1, beside), (3, both)):
        for m in range(piece.shape[0] // rows):
            at = pl.multiple_of(((index ^ m) * TEAM + (g ^ m_team)) * rows, rows)
            first, second = split(piece[m * rows : (m + 1) * rows])
            high[pl.ds(at, rows), :] = first
            low[pl.ds(at, rows), :] = second


def start_kernel(place, p0, p1, p2, p3, high, low, out, *sides):
    whole = team_order([p[...] for p in (p0, p1, p2, p3)], place[0])
    out[...] = product(whole[0], high[...], low[...], 1)
    for level, side in enumerate(sides):
        side[...] = whole[level + 1]


def couple_kernel(slot, place, own, got, side, high, low, total, out):
    total[...] = own[...] + got[...]
    out[...] = -product(total[...], high[...], low[...], 1)
    half = side.shape[1]
    at = pl.ds(pl.multiple_of(place[slot] * half, 128), half)
    out[:, at] = out[:, at] + side[...]


def forward_kernel(own, got, high, low, out):
    out[...] = product(own[...] + got[...], high[...], low[...], 1)


def backward_kernel(own, got, high, low, out):
    out[...] = product(own[...] + got[...], high[...], low[...], 0)


def carry_top_kernel(place, own, got, high, low, out, mine, total):
    total[...] = own[...] + got[...]
    out[...] = product(total[...], high[...], low[...], 0)
    half = mine.shape[1]
    mine[...] = total[:, pl.ds(pl.multiple_of(place[3] * half, 128), half)]


def subtract_kernel(solved, own, got, high, low, out):
    out[...] = product(solved[...] - (own[...] + got[...]), high[...], low[...], 0)


def carry_mid_kernel(place, own, got, top, high, low, out, *rest):
    pieces, total = rest[:-1], rest[-1]
    total[...] = own[...] + got[...]
    out[...] = product(total[...], high[...], low[...], 0)
    half = top.shape[1]
    mid = total[:, pl.ds(pl.multiple_of(place[2] * half, 128), half)]
    for level, value in enumerate((mid, top[...])):
        for piece, part in zip(pieces, team_pieces(value, place[0])):
            piece[level] = part


def finish_kernel(place, solved, own, got, high, low, *pieces):
    leaf = product(solved[...] - (own[...] + got[...]), high[...], low[...], 0)
    for piece, part in zip(pieces, team_pieces(leaf, place[0])):
        piece[...] = part


def output_kernel(place, *rest):
    leaf, upper, out, turned = rest[:TEAM], rest[TEAM : 2 * TEAM], rest[-2], rest[-1]
    width = leaf[0].shape[0]
    for m in range(TEAM):
        at = pl.ds(pl.multiple_of((place[0] ^ m) * width, 8), width)
        turned[0, at, :] = leaf[m][...]
        turned[1:, at, :] = upper[m][...]
    for level in range(out.shape[0]):
        out[level, 0] = turned[level].T


def local(
    right_sides,
    inverse_leaf,
    inverse_mid,
    inverse_top,
    coupling_mid,
    coupling_top,
    pattern_mid,
    pattern_top,
):
    front = lax.axis_size("front")
    cube_pos, front_pos = lax.axis_index("cube"), lax.axis_index("front")
    parts = front // TEAM
    levels, _, rows, columns = right_sides.shape
    width, half, full = columns // TEAM, TEAM * rows, front * rows
    group_mid, group_top = inverse_mid.shape[2] // full, inverse_top.shape[2] // full
    place = jnp.stack([front_pos % TEAM, front_pos // TEAM, cube_pos % group_mid, cube_pos % group_top])

    def to_parts(pieces, axis, unit):
        return [
            piece if m == 0 else exchange(piece, axis, m * unit)
            for m, piece in enumerate(pieces)
        ]

    def whole_block(own, across, slot):
        if across is None:
            across = exchange(own, "front", 2)
        beside = exchange(own, "front", 1)
        both = exchange(across, "front", 1)
        shape = (TEAM * own.shape[0], own.shape[1])
        return call(
            functools.partial(assemble, slot, rows), [(shape, BF16)] * 2,
            place, own, across, beside, both,
        )

    def partial_sum(value, axis, count, unit):
        got, bit = jnp.zeros_like(value), 1
        while bit < count:
            if bit > 1:
                value = value + got
            got = exchange(value, axis, bit * unit)
            bit *= 2
        return value, got

    out = call(
        prepare_leaf,
        [((rows, half), F32)] * parts + [((levels, width, rows), F32)] * TEAM,
        place, inverse_leaf, right_sides,
        scratch=[pltpu.VMEM((levels, columns, rows), F32)],
    )
    leaf_pieces, side_pieces = out[:parts], out[parts:]
    leaf_own = jnp.concatenate(to_parts(leaf_pieces, "front", TEAM))
    leaf_across = jnp.concatenate([
        exchange(piece, "front", m * TEAM + 2) for m, piece in enumerate(leaf_pieces)
    ])
    sides = to_parts(side_pieces, "front", 1)
    leaf = whole_block(leaf_own, leaf_across, 1)

    blocks = []
    for slot, count, coupling, pattern, inverse in (
        (2, group_mid, coupling_mid, pattern_mid, inverse_mid),
        (3, group_top, coupling_top, pattern_top, inverse_top),
    ):
        out = call(
            functools.partial(prepare_level, slot, count),
            [((rows, full), F32)] * count + [((rows, count * half), F32)] * parts,
            place, coupling, pattern, inverse,
        )
        couple_own = jnp.concatenate(to_parts(out[:count], "cube", 1))
        own = jnp.concatenate(to_parts(out[count:], "front", TEAM))
        blocks.append(whole_block(couple_own, None, slot))
        blocks.append(whole_block(own, None, 1))
    couple_mid, mid, couple_top, top = blocks

    vector = lambda n: ((width, n), F32)
    y0, side_mid, side_top = call(
        start_kernel, [vector(full), vector(half), vector(half)], place, *sides, *leaf,
    )
    y0 = partial_sum(y0, "front", parts, TEAM)
    y0, w1 = call(
        functools.partial(couple_kernel, 2), [vector(full), vector(group_mid * half)],
        place, *y0, side_mid, *couple_mid,
    )
    w1 = partial_sum(w1, "cube", group_mid, 1)
    y1, = call(forward_kernel, [vector(full)], *w1, *mid)
    y1 = partial_sum(y1, "front", parts, TEAM)
    y1, w2 = call(
        functools.partial(couple_kernel, 3), [vector(full), vector(group_top * half)],
        place, *y1, side_top, *couple_top,
    )
    w2 = partial_sum(w2, "cube", group_top, 1)
    y2, = call(forward_kernel, [vector(full)], *w2, *top)
    y2 = partial_sum(y2, "front", parts, TEAM)
    x2, = call(backward_kernel, [vector(group_top * half)], *y2, *top)
    x2 = partial_sum(x2, "cube", group_top, 1)
    c1, mine = call(
        carry_top_kernel, [vector(full), vector(half)], place, *x2, *couple_top,
        scratch=[pltpu.VMEM((width, group_top * half), F32)],
    )
    c1 = partial_sum(c1, "front", parts, TEAM)
    x1, = call(subtract_kernel, [vector(group_mid * half)], y1, *c1, *mid)
    x1 = partial_sum(x1, "cube", group_mid, 1)
    c0, *upper = call(
        carry_mid_kernel, [vector(full)] + [((2, width, rows), F32)] * TEAM,
        place, *x1, mine, *couple_mid,
        scratch=[pltpu.VMEM((width, group_mid * half), F32)],
    )
    c0 = partial_sum(c0, "front", parts, TEAM)
    upper = to_parts(upper, "front", 1)
    found = call(finish_kernel, [vector(rows)] * TEAM, place, y0, *c0, *leaf)
    found = to_parts(found, "front", 1)
    result, = call(
        output_kernel, [((levels, 1, rows, columns), F32)], place, *found, *upper,
        scratch=[pltpu.VMEM((levels, columns, rows), F32)],
    )
    return result


def solution(mesh):
    return jax.shard_map(
        local,
        mesh=mesh,
        in_specs=(
            P(None, "cube", "front", None),
            P("cube", "front", None),
            P("cube", "front", None),
            P("cube", "front", None),
            P("cube", "front", None),
            P("cube", "front", None),
            P("cube", "front", None),
            P("cube", "front", None),
        ),
        out_specs=P(None, "cube", "front", None),
        check_vma=False,
    )
```

time: 385 us -> 164 us (0.43)
  waiting for transfers between devices: 290 us -> 70.8 us
  Pallas kernels: 0 us -> 47.1 us
  blocking collectives: 29.6 us -> 0 us
  between operations: 14.4 us -> 0.38 us
  matrix products: 12.1 us -> 0 us
  starting transfers between devices: 22.7 us -> 32.1 us
    unnamed x9 -> x0, waiting for transfers between devices: 110 us -> none
    reduce_scatter x3 -> x0, waiting for transfers between devices: 103 us -> none  [spread_back(): lax.psum_scatter(jnp.einsum('rms,rn->smn', shaped, local_rows, precision=...]
    all_gather x2 -> x0, waiting for transfers between devices: 47.3 us -> none  [gathered_product(): lax.all_gather(stacked, 'front', axis=1, tiled=True)]
    pallas_call x0 -> x19, Pallas kernels: none -> 47.1 us  [call(): pl.pallas_call(kernel, out_shape=[jax.ShapeDtypeStruct(shape, dtype) for...]
    ppermute x12 -> x43, waiting for transfers between devices: 28.9 us -> 70.8 us  [exchange(): return lax.ppermute(value, axis, pairs)]
    all_gather x3 -> x0, blocking collectives: 29.6 us -> none  [gathered_product(): lax.all_gather(stacked, 'front', axis=1, tiled=True)]
    dot_general x10 -> x0, matrix products: 12.1 us -> none  [the longest x5 6.75 us: spread_back(): jnp.einsum('rms,rn->smn', shaped, local_rows, precision=lax.Precision.HIG...]
    ppermute x12 -> x43, starting transfers between devices: 22.3 us -> 32.1 us  [exchange(): return lax.ppermute(value, axis, pairs)]
  transfers between devices with their start and end apart: 19 -> 43, of which waited for: 19 -> 20; matrix products, arithmetic and copies ran while one was open for 1% -> 2% of each run, Pallas kernels for 0% -> 18%
where the time goes in v1:
time: 164 us; the launch traced here: 163 us
  waiting for transfers between devices  70.8 us (43%)
  Pallas kernels  47.1 us (29%)
  starting transfers between devices  32.1 us (20%)
  local copies, waits for them, and re-layouts  10.6 us (6%)
  other arithmetic  2.46 us (2%)
    ppermute x43, waiting for transfers between devices, exchange(): return lax.ppermute(value, axis, pairs)  70.8 us
    pallas_call x19, Pallas kernels, call(): pl.pallas_call(kernel, out_shape=[jax.ShapeDtypeStruct(shape, dtype) for...  47.1 us
    ppermute x43, starting transfers between devices, exchange(): return lax.ppermute(value, axis, pairs)  32.1 us
    unnamed x100, local copies, waits for them, and re-layouts  10.6 us
  transfers between devices with their start and end apart: 43, of which 20 were waited for; matrix products, arithmetic and copies ran while one was open for 2% of the time, Pallas kernels for 18%

profile of v1, /device:TPU:0, one launch (start us, length us, event | category | flops | bytes accessed | tf_op | source)
XLA Modules:
  0.0 163.5 jit_solution(6855179617867672968)
XLA Ops:
  0.6 1.8 %shard_map.82 = (f32[64,256]{1,0:T(8,128)}, f32[64,256]{1,0:T(8,128)}, f32[3,32,64]{2,1,0:T(8,128)}, f32[3,32,64]{2,1,0:T(8,128)}, f32[3,32,64]{2,1,0:T(8,128)}, /*index=5*/f32[3,32,64]{2,1,0:T(8,128)}) custom-call(s32[4]{0:T(128)} %pad_add_fusion.place, f32[1,64,512]{2,1,0:T(8,128)} %matrix.1, f32[3,1,64,128]{3,2,1,0:T(8,128)} %sides.1), custom_call_target="tpu_custom_call" | custom-call | tf_op jit(solution)/shard_map/pallas_call | solution.py:24
  2.4 3.9 %collective-permute-start.5 = (f32[64,256]{1,0:T(8,128)}, f32[64,256]{1,0:T(8,128)S(1)}, u32[]{:S(2)}, u32[]{:S(2)}) collective-permute-start(f32[64,256]{1,0:T(8,128)} %get-tuple-element.54), channel_id=1, source_target_pairs={{0,6},{1,7},{2,4},{3,5},{4,2},{5,3},{6,0},{7,1},{8,14},{9,15},{10,... | collective-permute-start | bytes 196616 | tf_op jit(solution)/shard_map/ppermute | solution.py:17
  6.8 2.4 %shard_map.90 = (f32[64,512]{1,0:T(8,128)}, f32[64,512]{1,0:T(8,128)}, f32[64,512]{1,0:T(8,128)}, f32[64,512]{1,0:T(8,128)}, f32[64,1024]{1,0:T(8,128)}, /*index=5*/f32[64,1024]{1,0:T(8,128)}) custom-call(s32[4]{0:T(128)} %pad_add_fusion.place, f32[1,64,2048]{2,1,0:T(8,128)} %coupling.3, s32[1,1,32]{2,1,0:T(1,128)} %pattern.3, f32[1,64,2048]{2,1,0:T(8,128)} %inverse.3), custom_call_target="tpu_custom_call" | custom-call | tf_op jit(solution)/shard_map/pallas_call | solution.py:24
  9.2 1.5 collective-permute-start.27
  10.7 1.6 collective-permute-start.19
  12.8 1.0 constant_dynamic-update-slice_fusion.13
  13.9 1.9 %shard_map.85 = (f32[64,512]{1,0:T(8,128)}, f32[64,512]{1,0:T(8,128)}, f32[64,512]{1,0:T(8,128)}, f32[64,512]{1,0:T(8,128)}) custom-call(s32[4]{0:T(128)} %pad_add_fusion.place, f32[1,64,1024]{2,1,0:T(8,128)} %coupling.2, s32[1,1,16]{2,1,0:T(1,128)} %pattern.2, f32[1,64,1024]{2,1,0:T(8,128)} %inverse.2), custom_call_target="tpu_custom_call" | custom-call | tf_op jit(solution)/shard_map/pallas_call | solution.py:24
  15.8 0.9 constant_dynamic-update-slice_fusion.7
  17.7 2.6 %collective-permute-start.20 = (f32[64,512]{1,0:T(8,128)S(1)}, f32[64,512]{1,0:T(8,128)S(1)}, u32[]{:S(2)}, u32[]{:S(2)}) collective-permute-start(f32[64,512]{1,0:T(8,128)S(1)} %copy-done.42), channel_id=1, source_target_pairs={{0,16},{8,24},{16,0},{24,8},{1,17},{9,25},{17,1},{25,9},{2,18},{10... | collective-permute-start | bytes 393224 | tf_op jit(solution)/shard_map/ppermute | solution.py:17
  22.0 7.2 %collective-permute-done.20 = f32[64,512]{1,0:T(8,128)S(1)} collective-permute-done((f32[64,512]{1,0:T(8,128)S(1)}, f32[64,512]{1,0:T(8,128)S(1)}, u32[]{:S(2)}, u32[]{:S(2)}) %collective-permute-start.20) | collective-permute-done | bytes 131104 | tf_op jit(solution)/shard_map/ppermute | solution.py:17
  29.2 1.2 collective-permute-done.p1
  31.0 1.6 collective-permute-start.22
  34.9 2.0 %shard_map.83 = (bf16[512,256]{1,0:T(8,128)(2,1)}, bf16[512,256]{1,0:T(8,128)(2,1)}) custom-call(s32[4]{0:T(128)} %pad_add_fusion.place, f32[128,256]{1,0:T(8,128)} %copy-done.10, f32[128,256]{1,0:T(8,128)} %copy-done.11, f32[128,256]{1,0:T(8,128)} %copy-done.17, f32[128,256]{1,0:T(8,128)} %copy-done.16), custom_call_target="tpu_custom_call" | custom-call | tf_op jit(solution)/shard_map/pallas_call | solution.py:24
  37.0 9.9 %collective-permute-done.1.p2 = f32[3,32,64]{2,1,0:T(8,128)S(1)} collective-permute-done((f32[3,32,64]{2,1,0:T(8,128)S(1)}, f32[3,32,64]{2,1,0:T(8,128)S(1)}, u32[]{:S(2)}, u32[]{:S(2)}) %collective-permute-start.1) | collective-permute-done | bytes 24608 | tf_op jit(solution)/shard_map/ppermute | solution.py:17
  47.0 1.5 collective-permute-start.10
  48.5 2.1 %shard_map.84 = (f32[32,512]{1,0:T(8,128)}, f32[32,256]{1,0:T(8,128)}, f32[32,256]{1,0:T(8,128)}) custom-call(s32[4]{0:T(128)} %pad_add_fusion.place, f32[3,32,64]{2,1,0:T(8,128)} %get-tuple-element.49.p0, f32[3,32,64]{2,1,0:T(8,128)} %copy-done.30, f32[3,32,64]{2,1,0:T(8,128)} %copy-done.31, f32[3,32,64]{2,1,0:T(8,128)} %copy-done.32, ...), custom_call_target="tpu_custom_call" | custom-call | tf_op jit(solution)/shard_map/pallas_call | solution.py:24
  51.2 4.1 %collective-permute-done.8.got = f32[32,512]{1,0:T(8,128)S(1)} collective-permute-done((f32[32,512]{1,0:T(8,128)}, f32[32,512]{1,0:T(8,128)S(1)}, u32[]{:S(2)}, u32[]{:S(2)}) %collective-permute-start.8) | collective-permute-done | bytes 65568 | tf_op jit(solution)/shard_map/ppermute | solution.py:17
  57.0 2.2 %collective-permute-done.10.across = f32[128,512]{1,0:T(8,128)S(1)} collective-permute-done((f32[128,512]{1,0:T(8,128)S(1)}, f32[128,512]{1,0:T(8,128)S(1)}, u32[]{:S(2)}, u32[]{:S(2)}) %collective-permute-start.10) | collective-permute-done | bytes 262176 | tf_op jit(solution)/shard_map/ppermute | solution.py:17
  59.7 1.2 collective-permute-done.12.both
  61.0 8.6 %collective-permute-done.28.across = f32[128,1024]{1,0:T(8,128)S(1)} collective-permute-done((f32[128,1024]{1,0:T(8,128)S(1)}, f32[128,1024]{1,0:T(8,128)S(1)}, u32[]{:S(2)}, u32[]{:S(2)}) %collective-permute-start.28) | collective-permute-done | bytes 524320 | tf_op jit(solution)/shard_map/ppermute | solution.py:17
  69.7 2.5 %shard_map.86 = (bf16[512,512]{1,0:T(8,128)(2,1)}, bf16[512,512]{1,0:T(8,128)(2,1)}) custom-call(s32[4]{0:T(128)} %pad_add_fusion.place, f32[128,512]{1,0:T(8,128)} %copy-done.2, f32[128,512]{1,0:T(8,128)} %copy-done.14, f32[128,512]{1,0:T(8,128)} %copy-done.15, f32[128,512]{1,0:T(8,128)} %collective-permute-done.12.both), custom_call_target="tpu_custom_call" | custom-call | tf_op jit(solution)/shard_map/pallas_call | solution.py:24
  72.2 2.5 %shard_map.87 = (f32[32,512]{1,0:T(8,128)}, f32[32,512]{1,0:T(8,128)}) custom-call(s32[4]{0:T(128)} %pad_add_fusion.place, f32[32,512]{1,0:T(8,128)} %get-tuple-element.57.own, f32[32,512]{1,0:T(8,128)} %copy-done.22, f32[32,256]{1,0:T(8,128)} %get-tuple-element.58.side, bf16[512,512]{1,0:T(8,128)(2,1)} %get-tuple-element.61.high, ...), custom_call_target="tpu_custom_call" | custom-call | tf_op jit(solution)/shard_map/pallas_call | solution.py:24
  75.4 2.3 %shard_map.88 = (bf16[512,512]{1,0:T(8,128)(2,1)}, bf16[512,512]{1,0:T(8,128)(2,1)}) custom-call(s32[4]{0:T(128)} %pad_add_fusion.place, f32[128,512]{1,0:T(8,128)} %copy-done.3, f32[128,512]{1,0:T(8,128)} %copy-done.12, f32[128,512]{1,0:T(8,128)} %copy-done.13, f32[128,512]{1,0:T(8,128)} %collective-permute-done.17.both), custom_call_target="tpu_custom_call" | custom-call | tf_op jit(solution)/shard_map/pallas_call | solution.py:24
  77.7 1.6 collective-permute-done.13.got
  79.9 2.5 %shard_map.89.own = f32[32,512]{1,0:T(8,128)} custom-call(f32[32,512]{1,0:T(8,128)} %get-tuple-element.64.own, f32[32,512]{1,0:T(8,128)} %copy-done.26, bf16[512,512]{1,0:T(8,128)(2,1)} %get-tuple-element.67.high, bf16[512,512]{1,0:T(8,128)(2,1)} %get-tuple-element.68.low), custom_call_target="tpu_custom_call" | custom-call | tf_op jit(solution)/shard_map/pallas_call | solution.py:24
  82.7 3.1 %shard_map.91 = (bf16[1024,512]{1,0:T(8,128)(2,1)}, bf16[1024,512]{1,0:T(8,128)(2,1)}) custom-call(s32[4]{0:T(128)} %pad_add_fusion.place, f32[256,512]{1,0:T(8,128)} %copy-done.1, f32[256,512]{1,0:T(8,128)} %copy-done.4, f32[256,512]{1,0:T(8,128)} %collective-permute-done.23.beside, f32[256,512]{1,0:T(8,128)} %collective-permute-done.24.both), custom_call_target="tpu_custom_call" | custom-call | tf_op jit(solution)/shard_map/pallas_call | solution.py:24
  85.7 1.1 collective-permute-done.18.got
  87.5 3.3 %shard_map.92 = (f32[32,512]{1,0:T(8,128)}, f32[32,1024]{1,0:T(8,128)}) custom-call(s32[4]{0:T(128)} %pad_add_fusion.place, f32[32,512]{1,0:T(8,128)} %shard_map.89.own, f32[32,512]{1,0:T(8,128)} %copy-done.24, f32[32,256]{1,0:T(8,128)} %get-tuple-element.69.side, bf16[1024,512]{1,0:T(8,128)(2,1)} %get-tuple-element.74.high, ...), custom_call_target="tpu_custom_call" | custom-call | tf_op jit(solution)/shard_map/pallas_call | solution.py:24
  91.5 4.5 %collective-permute-done.25 = f32[32,1024]{1,0:T(8,128)S(1)} collective-permute-done((f32[32,1024]{1,0:T(8,128)}, f32[32,1024]{1,0:T(8,128)S(1)}, u32[]{:S(2)}, u32[]{:S(2)}) %collective-permute-start.25) | collective-permute-done | bytes 131104 | tf_op jit(solution)/shard_map/ppermute | solution.py:17
  96.9 1.9 %collective-permute-start.26 = (f32[32,1024]{1,0:T(8,128)S(1)}, f32[32,1024]{1,0:T(8,128)S(1)}, u32[]{:S(2)}, u32[]{:S(2)}) collective-permute-start(f32[32,1024]{1,0:T(8,128)S(1)} %add.20.own), channel_id=1, source_target_pairs={{0,16},{8,24},{16,0},{24,8},{1,17},{9,25},{17,1},{25,9},{2,18},{10... | collective-permute-start | bytes 393224 | tf_op jit(solution)/shard_map/ppermute | solution.py:17
  100.4 3.2 %shard_map.93 = (bf16[512,1024]{1,0:T(8,128)(2,1)}, bf16[512,1024]{1,0:T(8,128)(2,1)}) custom-call(s32[4]{0:T(128)} %pad_add_fusion.place, f32[128,1024]{1,0:T(8,128)} %copy-done, f32[128,1024]{1,0:T(8,128)} %copy-done.5, f32[128,1024]{1,0:T(8,128)} %copy-done.6, f32[128,1024]{1,0:T(8,128)} %copy-done.7), custom_call_target="tpu_custom_call" | custom-call | tf_op jit(solution)/shard_map/pallas_call | solution.py:24
  104.9 3.3 %shard_map.94.own = f32[32,512]{1,0:T(8,128)} custom-call(f32[32,1024]{1,0:T(8,128)} %copy-done.8, f32[32,1024]{1,0:T(8,128)} %copy-done.18, bf16[512,1024]{1,0:T(8,128)(2,1)} %get-tuple-element.80.high, bf16[512,1024]{1,0:T(8,128)(2,1)} %get-tuple-element.81.low), custom_call_target="tpu_custom_call" | custom-call | tf_op jit(solution)/shard_map/pallas_call | solution.py:24
  108.9 3.8 %collective-permute-done.31.got = f32[32,512]{1,0:T(8,128)S(1)} collective-permute-done((f32[32,512]{1,0:T(8,128)}, f32[32,512]{1,0:T(8,128)S(1)}, u32[]{:S(2)}, u32[]{:S(2)}) %collective-permute-start.31) | collective-permute-done | bytes 65568 | tf_op jit(solution)/shard_map/ppermute | solution.py:17
  113.3 2.9 %shard_map.95 = f32[32,1024]{1,0:T(8,128)} custom-call(f32[32,512]{1,0:T(8,128)} %shard_map.94.own, f32[32,512]{1,0:T(8,128)} %copy-done.28, bf16[512,1024]{1,0:T(8,128)(2,1)} %get-tuple-element.80.high, bf16[512,1024]{1,0:T(8,128)(2,1)} %get-tuple-element.81.low), custom_call_target="tpu_custom_call" | custom-call | tf_op jit(solution)/shard_map/pallas_call | solution.py:24
  116.9 5.8 %collective-permute-done.32 = f32[32,1024]{1,0:T(8,128)S(1)} collective-permute-done((f32[32,1024]{1,0:T(8,128)}, f32[32,1024]{1,0:T(8,128)S(1)}, u32[]{:S(2)}, u32[]{:S(2)}) %collective-permute-start.32) | collective-permute-done | bytes 131104 | tf_op jit(solution)/shard_map/ppermute | solution.py:17
  123.6 1.2 collective-permute-start.33
  124.8 5.8 %collective-permute-done.33.got = f32[32,1024]{1,0:T(8,128)S(1)} collective-permute-done((f32[32,1024]{1,0:T(8,128)S(1)}, f32[32,1024]{1,0:T(8,128)S(1)}, u32[]{:S(2)}, u32[]{:S(2)}) %collective-permute-start.33) | collective-permute-done | bytes 131104 | tf_op jit(solution)/shard_map/ppermute | solution.py:17
  131.3 3.0 %shard_map.96 = (f32[32,512]{1,0:T(8,128)}, f32[32,256]{1,0:T(8,128)}) custom-call(s32[4]{0:T(128)} %pad_add_fusion.place, f32[32,1024]{1,0:T(8,128)} %copy-done.9, f32[32,1024]{1,0:T(8,128)} %copy-done.19, bf16[1024,512]{1,0:T(8,128)(2,1)} %get-tuple-element.74.high, bf16[1024,512]{1,0:T(8,128)(2,1)} %get-tuple-element.75.low), custom_call_target="tpu_custom_call" | custom-call | tf_op jit(solution)/shard_map/pallas_call | solution.py:24
  135.1 3.7 %collective-permute-done.34.got = f32[32,512]{1,0:T(8,128)S(1)} collective-permute-done((f32[32,512]{1,0:T(8,128)}, f32[32,512]{1,0:T(8,128)S(1)}, u32[]{:S(2)}, u32[]{:S(2)}) %collective-permute-start.34) | collective-permute-done | bytes 65568 | tf_op jit(solution)/shard_map/ppermute | solution.py:17
  139.4 2.3 %shard_map.97.own = f32[32,512]{1,0:T(8,128)} custom-call(f32[32,512]{1,0:T(8,128)} %get-tuple-element.76.solved, f32[32,512]{1,0:T(8,128)} %get-tuple-element.82.own, f32[32,512]{1,0:T(8,128)} %copy-done.27, bf16[512,512]{1,0:T(8,128)(2,1)} %get-tuple-element.67.high, bf16[512,512]{1,0:T(8,128)(2,1)} %get-tuple-element.68.low), custom_call_target="tpu_custom_call" | custom-call | tf_op jit(solution)/shard_map/pallas_call | solution.py:24
  141.6 4.5 %collective-permute-done.35.got = f32[32,512]{1,0:T(8,128)S(1)} collective-permute-done((f32[32,512]{1,0:T(8,128)}, f32[32,512]{1,0:T(8,128)S(1)}, u32[]{:S(2)}, u32[]{:S(2)}) %collective-permute-start.35) | collective-permute-done | bytes 65568 | tf_op jit(solution)/shard_map/ppermute | solution.py:17
  146.7 2.3 %shard_map.98 = (f32[32,512]{1,0:T(8,128)}, f32[2,32,64]{2,1,0:T(8,128)}, f32[2,32,64]{2,1,0:T(8,128)}, f32[2,32,64]{2,1,0:T(8,128)}, f32[2,32,64]{2,1,0:T(8,128)}) custom-call(s32[4]{0:T(128)} %pad_add_fusion.place, f32[32,512]{1,0:T(8,128)} %shard_map.97.own, f32[32,512]{1,0:T(8,128)} %copy-done.25, f32[32,256]{1,0:T(8,128)} %get-tuple-element.83.top, ...), custom_call_target="tpu_custom_call" | custom-call | tf_op jit(solution)/shard_map/pallas_call | solution.py:24
  149.8 1.5 collective-permute-start.41
  151.7 1.8 %collective-permute-done.36.got = f32[32,512]{1,0:T(8,128)S(1)} collective-permute-done((f32[32,512]{1,0:T(8,128)}, f32[32,512]{1,0:T(8,128)S(1)}, u32[]{:S(2)}, u32[]{:S(2)}) %collective-permute-start.36) | collective-permute-done | bytes 65568 | tf_op jit(solution)/shard_map/ppermute | solution.py:17
  154.2 2.1 %shard_map.99 = (f32[32,64]{1,0:T(8,128)}, f32[32,64]{1,0:T(8,128)}, f32[32,64]{1,0:T(8,128)}, f32[32,64]{1,0:T(8,128)}) custom-call(s32[4]{0:T(128)} %pad_add_fusion.place, f32[32,512]{1,0:T(8,128)} %get-tuple-element.63.solved, f32[32,512]{1,0:T(8,128)} %get-tuple-element.84.own, f32[32,512]{1,0:T(8,128)} %copy-done.23, ...), custom_call_target="tpu_custom_call" | custom-call | tf_op jit(solution)/shard_map/pallas_call | solution.py:24
  156.3 1.5 collective-permute-start.38
  158.2 2.1 %collective-permute-done.38.rest_2_ = f32[32,64]{1,0:T(8,128)S(1)} collective-permute-done((f32[32,64]{1,0:T(8,128)}, f32[32,64]{1,0:T(8,128)S(1)}, u32[]{:S(2)}, u32[]{:S(2)}) %collective-permute-start.38) | collective-permute-done | bytes 8224 | tf_op jit(solution)/shard_map/ppermute | solution.py:17
  161.8 1.7 %shard_map.100 = f32[3,1,64,128]{3,2,1,0:T(8,128)} custom-call(s32[4]{0:T(128)} %pad_add_fusion.place, f32[32,64]{1,0:T(8,128)} %get-tuple-element.85.rest_0_, f32[32,64]{1,0:T(8,128)} %copy-done.36, f32[32,64]{1,0:T(8,128)} %copy-done.37, f32[32,64]{1,0:T(8,128)} %copy-done.38, f32[2,32,64]{2,1,0:T(8,128)} %get-tuple-element.89.rest_4_, ...), custom_call_target="tpu_custom_call" | custom-call | tf_op jit(solution)/shard_map/pallas_call | solution.py:24
  (166 shorter events, 26.1 us)
Async XLA Ops:
  2.4 17.9 %collective-permute-start.5 = (f32[64,256]{1,0:T(8,128)}, f32[64,256]{1,0:T(8,128)S(1)}, u32[]{:S(2)}, u32[]{:S(2)}) collective-permute-start(f32[64,256]{1,0:T(8,128)} %get-tuple-element.54), channel_id=1, source_target_pairs={{0,6},{1,7},{2,4},{3,5},{4,2},{5,3},{6,0},{7,1},{8,14},{9,15},{10,... | collective-permute-start | bytes 196616 | tf_op jit(solution)/shard_map/ppermute | solution.py:17
  6.3 14.3 %collective-permute-start.3 = (f32[64,256]{1,0:T(8,128)}, f32[64,256]{1,0:T(8,128)S(1)}, u32[]{:S(2)}, u32[]{:S(2)}) collective-permute-start(f32[64,256]{1,0:T(8,128)} %get-tuple-element.54), channel_id=1, source_target_pairs={{0,4},{1,5},{2,6},{3,7},{4,0},{5,1},{6,2},{7,3},{8,12},{9,13},{10,... | collective-permute-start | bytes 196616 | tf_op jit(solution)/shard_map/ppermute | solution.py:17
  9.2 41.5 %collective-permute-start.27 = (f32[64,1024]{1,0:T(8,128)}, f32[64,1024]{1,0:T(8,128)S(1)}, u32[]{:S(2)}, u32[]{:S(2)}) collective-permute-start(f32[64,1024]{1,0:T(8,128)} %get-tuple-element.79), channel_id=1, source_target_pairs={{0,4},{1,5},{2,6},{3,7},{4,0},{5,1},{6,2},{7,3},{8,12},{9,13},{10,... | collective-permute-start | bytes 786440 | tf_op jit(solution)/shard_map/ppermute | solution.py:17
  10.7 10.3 %collective-permute-start.19 = (f32[64,512]{1,0:T(8,128)}, f32[64,512]{1,0:T(8,128)S(1)}, u32[]{:S(2)}, u32[]{:S(2)}) collective-permute-start(f32[64,512]{1,0:T(8,128)} %get-tuple-element.71), channel_id=1, source_target_pairs={{0,8},{8,0},{16,24},{24,16},{1,9},{9,1},{17,25},{25,17},{2,10},{10... | collective-permute-start | bytes 393224 | tf_op jit(solution)/shard_map/ppermute | solution.py:17
  12.3 4.5 %collective-permute-start.4 = (f32[64,256]{1,0:T(8,128)S(1)}, f32[64,256]{1,0:T(8,128)S(1)}, u32[]{:S(2)}, u32[]{:S(2)}) collective-permute-start(f32[64,256]{1,0:T(8,128)S(1)} %copy-done.29), channel_id=1, source_target_pairs={{0,2},{1,3},{2,0},{3,1},{4,6},{5,7},{6,4},{7,5},{8,10},{9,11},{10,... | collective-permute-start | bytes 196616 | tf_op jit(solution)/shard_map/ppermute | solution.py:17
  17.7 11.5 %collective-permute-start.20 = (f32[64,512]{1,0:T(8,128)S(1)}, f32[64,512]{1,0:T(8,128)S(1)}, u32[]{:S(2)}, u32[]{:S(2)}) collective-permute-start(f32[64,512]{1,0:T(8,128)S(1)} %copy-done.42), channel_id=1, source_target_pairs={{0,16},{8,24},{16,0},{24,8},{1,17},{9,25},{17,1},{25,9},{2,18},{10... | collective-permute-start | bytes 393224 | tf_op jit(solution)/shard_map/ppermute | solution.py:17
  20.3 10.2 %collective-permute-start.21 = (f32[64,512]{1,0:T(8,128)S(1)}, f32[64,512]{1,0:T(8,128)S(1)}, u32[]{:S(2)}, u32[]{:S(2)}) collective-permute-start(f32[64,512]{1,0:T(8,128)S(1)} %copy-done.39), channel_id=1, source_target_pairs={{0,24},{8,16},{16,8},{24,0},{1,25},{9,17},{17,9},{25,1},{2,26},{10... | collective-permute-start | bytes 393224 | tf_op jit(solution)/shard_map/ppermute | solution.py:17
  20.6 10.4 %collective-permute-start.14 = (f32[64,512]{1,0:T(8,128)S(1)}, f32[64,512]{1,0:T(8,128)S(1)}, u32[]{:S(2)}, u32[]{:S(2)}) collective-permute-start(f32[64,512]{1,0:T(8,128)S(1)} %copy-done.41), channel_id=1, source_target_pairs={{0,4},{1,5},{2,6},{3,7},{4,0},{5,1},{6,2},{7,3},{8,12},{9,13},{10,... | collective-permute-start | bytes 393224 | tf_op jit(solution)/shard_map/ppermute | solution.py:17
  21.2 11.4 %collective-permute-start.9 = (f32[64,512]{1,0:T(8,128)S(1)}, f32[64,512]{1,0:T(8,128)S(1)}, u32[]{:S(2)}, u32[]{:S(2)}) collective-permute-start(f32[64,512]{1,0:T(8,128)S(1)} %copy-done.40), channel_id=1, source_target_pairs={{0,8},{8,0},{16,24},{24,16},{1,9},{9,1},{17,25},{25,17},{2,10},{10... | collective-permute-start | bytes 393224 | tf_op jit(solution)/shard_map/ppermute | solution.py:17
  29.2 1.2 collective-permute-start
  30.4 2.9 %collective-permute-start.7 = (f32[128,256]{1,0:T(8,128)S(1)}, f32[128,256]{1,0:T(8,128)S(1)}, u32[]{:S(2)}, u32[]{:S(2)}) collective-permute-start(f32[128,256]{1,0:T(8,128)S(1)} %constant_dynamic-update-slice_fusion.2.across), channel_id=1, source_target_pairs={{0,1},{1,0},{2,3},{3,2},{4,5},{5,4},{6,7},{7,6},{8,9},{9,8},{10,11... | collective-permute-start | bytes 393224 | tf_op jit(solution)/shard_map/ppermute | solution.py:17
  30.6 3.4 %collective-permute-start.6 = (f32[128,256]{1,0:T(8,128)S(1)}, f32[128,256]{1,0:T(8,128)S(1)}, u32[]{:S(2)}, u32[]{:S(2)}) collective-permute-start(f32[128,256]{1,0:T(8,128)S(1)} %constant_dynamic-update-slice_fusion.own), channel_id=1, source_target_pairs={{0,1},{1,0},{2,3},{3,2},{4,5},{5,4},{6,7},{7,6},{8,9},{9,8},{10,11... | collective-permute-start | bytes 393224 | tf_op jit(solution)/shard_map/ppermute | solution.py:17
  31.0 25.4 %copy-start.1 = (f32[256,512]{1,0:T(8,128)}, f32[256,512]{1,0:T(8,128)S(1)}, u32[]{:S(2)}) copy-start(f32[256,512]{1,0:T(8,128)S(1)} %constant_dynamic-update-slice_fusion.8.own) | copy-start | bytes 1572868
  31.0 25.9 %collective-permute-start.22 = (f32[256,512]{1,0:T(8,128)S(1)}, f32[256,512]{1,0:T(8,128)S(1)}, u32[]{:S(2)}, u32[]{:S(2)}) collective-permute-start(f32[256,512]{1,0:T(8,128)S(1)} %constant_dynamic-update-slice_fusion.8.own), channel_id=1, source_target_pairs={{0,2},{1,3},{2,0},{3,1},{4,6},{5,7},{6,4},{7,5},{8,10},{9,11},{10,... | collective-permute-start | bytes 1572872 | tf_op jit(solution)/shard_map/ppermute | solution.py:17
  32.6 14.3 %collective-permute-start.1 = (f32[3,32,64]{2,1,0:T(8,128)S(1)}, f32[3,32,64]{2,1,0:T(8,128)S(1)}, u32[]{:S(2)}, u32[]{:S(2)}) collective-permute-start(f32[3,32,64]{2,1,0:T(8,128)S(1)} %copy-done.44), channel_id=1, source_target_pairs={{0,2},{1,3},{2,0},{3,1},{4,6},{5,7},{6,4},{7,5},{8,10},{9,11},{10,... | collective-permute-start | bytes 73736 | tf_op jit(solution)/shard_map/ppermute | solution.py:17
  33.3 13.7 %collective-permute-start.2 = (f32[3,32,64]{2,1,0:T(8,128)S(1)}, f32[3,32,64]{2,1,0:T(8,128)S(1)}, u32[]{:S(2)}, u32[]{:S(2)}) collective-permute-start(f32[3,32,64]{2,1,0:T(8,128)S(1)} %copy-done.43), channel_id=1, source_target_pairs={{0,3},{1,2},{2,1},{3,0},{4,7},{5,6},{6,5},{7,4},{8,11},{9,10},{10,... | collective-permute-start | bytes 73736 | tf_op jit(solution)/shard_map/ppermute | solution.py:17
  34.0 22.3 %collective-permute-start.15 = (f32[128,512]{1,0:T(8,128)S(1)}, f32[128,512]{1,0:T(8,128)S(1)}, u32[]{:S(2)}, u32[]{:S(2)}) collective-permute-start(f32[128,512]{1,0:T(8,128)S(1)} %constant_dynamic-update-slice_fusion.6.own), channel_id=1, source_target_pairs={{0,2},{1,3},{2,0},{3,1},{4,6},{5,7},{6,4},{7,5},{8,10},{9,11},{10,... | collective-permute-start | bytes 786440 | tf_op jit(solution)/shard_map/ppermute | solution.py:17
  34.9 21.3 %copy-start.2 = (f32[128,512]{1,0:T(8,128)}, f32[128,512]{1,0:T(8,128)S(1)}, u32[]{:S(2)}) copy-start(f32[128,512]{1,0:T(8,128)S(1)} %constant_dynamic-update-slice_fusion.4.own) | copy-start | bytes 786436
  46.9 9.4 %collective-permute-start.16 = (f32[128,512]{1,0:T(8,128)S(1)}, f32[128,512]{1,0:T(8,128)S(1)}, u32[]{:S(2)}, u32[]{:S(2)}) collective-permute-start(f32[128,512]{1,0:T(8,128)S(1)} %constant_dynamic-update-slice_fusion.6.own), channel_id=1, source_target_pairs={{0,1},{1,0},{2,3},{3,2},{4,5},{5,4},{6,7},{7,6},{8,9},{9,8},{10,11... | collective-permute-start | bytes 786440 | tf_op jit(solution)/shard_map/ppermute | solution.py:17
  47.0 12.2 %collective-permute-start.10 = (f32[128,512]{1,0:T(8,128)S(1)}, f32[128,512]{1,0:T(8,128)S(1)}, u32[]{:S(2)}, u32[]{:S(2)}) collective-permute-start(f32[128,512]{1,0:T(8,128)S(1)} %constant_dynamic-update-slice_fusion.4.own), channel_id=1, source_target_pairs={{0,2},{1,3},{2,0},{3,1},{4,6},{5,7},{6,4},{7,5},{8,10},{9,11},{10,... | collective-permute-start | bytes 786440 | tf_op jit(solution)/shard_map/ppermute | solution.py:17
  50.7 4.7 %collective-permute-start.8 = (f32[32,512]{1,0:T(8,128)}, f32[32,512]{1,0:T(8,128)S(1)}, u32[]{:S(2)}, u32[]{:S(2)}) collective-permute-start(f32[32,512]{1,0:T(8,128)} %get-tuple-element.57.own), channel_id=1, source_target_pairs={{0,4},{1,5},{2,6},{3,7},{4,0},{5,1},{6,2},{7,3},{8,12},{9,13},{10,... | collective-permute-start | bytes 196616 | tf_op jit(solution)/shard_map/ppermute | solution.py:17
  51.2 20.9 %copy-start = (f32[128,1024]{1,0:T(8,128)}, f32[128,1024]{1,0:T(8,128)S(1)}, u32[]{:S(2)}) copy-start(f32[128,1024]{1,0:T(8,128)S(1)} %constant_dynamic-update-slice_fusion.12.own) | copy-start | bytes 1572868
  55.4 16.8 %copy-start.22 = (f32[32,512]{1,0:T(8,128)}, f32[32,512]{1,0:T(8,128)S(1)}, u32[]{:S(2)}) copy-start(f32[32,512]{1,0:T(8,128)S(1)} %collective-permute-done.8.got) | copy-start | bytes 196612
  55.4 14.3 %collective-permute-start.28 = (f32[128,1024]{1,0:T(8,128)S(1)}, f32[128,1024]{1,0:T(8,128)S(1)}, u32[]{:S(2)}, u32[]{:S(2)}) collective-permute-start(f32[128,1024]{1,0:T(8,128)S(1)} %constant_dynamic-update-slice_fusion.12.own), channel_id=1, source_target_pairs={{0,2},{1,3},{2,0},{3,1},{4,6},{5,7},{6,4},{7,5},{8,10},{9,11},{10,... | collective-permute-start | bytes 1572872 | tf_op jit(solution)/shard_map/ppermute | solution.py:17
  56.3 18.4 %copy-start.12 = (f32[128,512]{1,0:T(8,128)}, f32[128,512]{1,0:T(8,128)S(1)}, u32[]{:S(2)}) copy-start(f32[128,512]{1,0:T(8,128)S(1)} %collective-permute-done.15.across) | copy-start | bytes 786436
  56.3 2.9 %collective-permute-start.11 = (f32[128,512]{1,0:T(8,128)S(1)}, f32[128,512]{1,0:T(8,128)S(1)}, u32[]{:S(2)}, u32[]{:S(2)}) collective-permute-start(f32[128,512]{1,0:T(8,128)S(1)} %constant_dynamic-update-slice_fusion.4.own), channel_id=1, source_target_pairs={{0,1},{1,0},{2,3},{3,2},{4,5},{5,4},{6,7},{7,6},{8,9},{9,8},{10,11... | collective-permute-start | bytes 786440 | tf_op jit(solution)/shard_map/ppermute | solution.py:17
  56.4 26.3 %collective-permute-start.23 = (f32[256,512]{1,0:T(8,128)S(1)}, f32[256,512]{1,0:T(8,128)}, u32[]{:S(2)}, u32[]{:S(2)}) collective-permute-start(f32[256,512]{1,0:T(8,128)S(1)} %constant_dynamic-update-slice_fusion.8.own), channel_id=1, source_target_pairs={{0,1},{1,0},{2,3},{3,2},{4,5},{5,4},{6,7},{7,6},{8,9},{9,8},{10,11... | collective-permute-start | bytes 1572872 | tf_op jit(solution)/shard_map/ppermute | solution.py:17
  56.9 25.7 %collective-permute-start.24 = (f32[256,512]{1,0:T(8,128)S(1)}, f32[256,512]{1,0:T(8,128)}, u32[]{:S(2)}, u32[]{:S(2)}) collective-permute-start(f32[256,512]{1,0:T(8,128)S(1)} %collective-permute-done.22.across), channel_id=1, source_target_pairs={{0,1},{1,0},{2,3},{3,2},{4,5},{5,4},{6,7},{7,6},{8,9},{9,8},{10,11... | collective-permute-start | bytes 1572872 | tf_op jit(solution)/shard_map/ppermute | solution.py:17
  59.2 1.7 %collective-permute-start.12 = (f32[128,512]{1,0:T(8,128)S(1)}, f32[128,512]{1,0:T(8,128)}, u32[]{:S(2)}, u32[]{:S(2)}) collective-permute-start(f32[128,512]{1,0:T(8,128)S(1)} %collective-permute-done.10.across), channel_id=1, source_target_pairs={{0,1},{1,0},{2,3},{3,2},{4,5},{5,4},{6,7},{7,6},{8,9},{9,8},{10,11... | collective-permute-start | bytes 786440 | tf_op jit(solution)/shard_map/ppermute | solution.py:17
  59.2 15.4 %collective-permute-start.17 = (f32[128,512]{1,0:T(8,128)S(1)}, f32[128,512]{1,0:T(8,128)}, u32[]{:S(2)}, u32[]{:S(2)}) collective-permute-start(f32[128,512]{1,0:T(8,128)S(1)} %collective-permute-done.15.across), channel_id=1, source_target_pairs={{0,1},{1,0},{2,3},{3,2},{4,5},{5,4},{6,7},{7,6},{8,9},{9,8},{10,11... | collective-permute-start | bytes 786440 | tf_op jit(solution)/shard_map/ppermute | solution.py:17
  60.9 37.9 %collective-permute-start.29 = (f32[128,1024]{1,0:T(8,128)S(1)}, f32[128,1024]{1,0:T(8,128)S(1)}, u32[]{:S(2)}, u32[]{:S(2)}) collective-permute-start(f32[128,1024]{1,0:T(8,128)S(1)} %constant_dynamic-update-slice_fusion.12.own), channel_id=1, source_target_pairs={{0,1},{1,0},{2,3},{3,2},{4,5},{5,4},{6,7},{7,6},{8,9},{9,8},{10,11... | collective-permute-start | bytes 1572872 | tf_op jit(solution)/shard_map/ppermute | solution.py:17
  69.7 29.1 %collective-permute-start.30 = (f32[128,1024]{1,0:T(8,128)S(1)}, f32[128,1024]{1,0:T(8,128)S(1)}, u32[]{:S(2)}, u32[]{:S(2)}) collective-permute-start(f32[128,1024]{1,0:T(8,128)S(1)} %collective-permute-done.28.across), channel_id=1, source_target_pairs={{0,1},{1,0},{2,3},{3,2},{4,5},{5,4},{6,7},{7,6},{8,9},{9,8},{10,11... | collective-permute-start | bytes 1572872 | tf_op jit(solution)/shard_map/ppermute | solution.py:17
  74.7 4.6 %collective-permute-start.13 = (f32[32,512]{1,0:T(8,128)}, f32[32,512]{1,0:T(8,128)S(1)}, u32[]{:S(2)}, u32[]{:S(2)}) collective-permute-start(f32[32,512]{1,0:T(8,128)} %get-tuple-element.64.own), channel_id=1, source_target_pairs={{0,8},{8,0},{16,24},{24,16},{1,9},{9,1},{17,25},{25,17},{2,10},{10... | collective-permute-start | bytes 196616 | tf_op jit(solution)/shard_map/ppermute | solution.py:17
  82.3 4.5 %collective-permute-start.18 = (f32[32,512]{1,0:T(8,128)}, f32[32,512]{1,0:T(8,128)S(1)}, u32[]{:S(2)}, u32[]{:S(2)}) collective-permute-start(f32[32,512]{1,0:T(8,128)} %shard_map.89.own), channel_id=1, source_target_pairs={{0,4},{1,5},{2,6},{3,7},{4,0},{5,1},{6,2},{7,3},{8,12},{9,13},{10,... | collective-permute-start | bytes 196616 | tf_op jit(solution)/shard_map/ppermute | solution.py:17
  90.8 5.2 %collective-permute-start.25 = (f32[32,1024]{1,0:T(8,128)}, f32[32,1024]{1,0:T(8,128)S(1)}, u32[]{:S(2)}, u32[]{:S(2)}) collective-permute-start(f32[32,1024]{1,0:T(8,128)} %get-tuple-element.77), channel_id=1, source_target_pairs={{0,8},{8,0},{16,24},{24,16},{1,9},{9,1},{17,25},{25,17},{2,10},{10... | collective-permute-start | bytes 393224 | tf_op jit(solution)/shard_map/ppermute | solution.py:17
  96.9 7.3 %collective-permute-start.26 = (f32[32,1024]{1,0:T(8,128)S(1)}, f32[32,1024]{1,0:T(8,128)S(1)}, u32[]{:S(2)}, u32[]{:S(2)}) collective-permute-start(f32[32,1024]{1,0:T(8,128)S(1)} %add.20.own), channel_id=1, source_target_pairs={{0,16},{8,24},{16,0},{24,8},{1,17},{9,25},{17,1},{25,9},{2,18},{10... | collective-permute-start | bytes 393224 | tf_op jit(solution)/shard_map/ppermute | solution.py:17
  108.2 4.5 %collective-permute-start.31 = (f32[32,512]{1,0:T(8,128)}, f32[32,512]{1,0:T(8,128)S(1)}, u32[]{:S(2)}, u32[]{:S(2)}) collective-permute-start(f32[32,512]{1,0:T(8,128)} %shard_map.94.own), channel_id=1, source_target_pairs={{0,4},{1,5},{2,6},{3,7},{4,0},{5,1},{6,2},{7,3},{8,12},{9,13},{10,... | collective-permute-start | bytes 196616 | tf_op jit(solution)/shard_map/ppermute | solution.py:17
  116.3 6.4 %collective-permute-start.32 = (f32[32,1024]{1,0:T(8,128)}, f32[32,1024]{1,0:T(8,128)S(1)}, u32[]{:S(2)}, u32[]{:S(2)}) collective-permute-start(f32[32,1024]{1,0:T(8,128)} %shard_map.95), channel_id=1, source_target_pairs={{0,8},{8,0},{16,24},{24,16},{1,9},{9,1},{17,25},{25,17},{2,10},{10... | collective-permute-start | bytes 393224 | tf_op jit(solution)/shard_map/ppermute | solution.py:17
  123.6 7.0 %collective-permute-start.33 = (f32[32,1024]{1,0:T(8,128)S(1)}, f32[32,1024]{1,0:T(8,128)S(1)}, u32[]{:S(2)}, u32[]{:S(2)}) collective-permute-start(f32[32,1024]{1,0:T(8,128)S(1)} %add.21.own), channel_id=1, source_target_pairs={{0,16},{8,24},{16,0},{24,8},{1,17},{9,25},{17,1},{25,9},{2,18},{10... | collective-permute-start | bytes 393224 | tf_op jit(solution)/shard_map/ppermute | solution.py:17
  134.3 4.5 %collective-permute-start.34 = (f32[32,512]{1,0:T(8,128)}, f32[32,512]{1,0:T(8,128)S(1)}, u32[]{:S(2)}, u32[]{:S(2)}) collective-permute-start(f32[32,512]{1,0:T(8,128)} %get-tuple-element.82.own), channel_id=1, source_target_pairs={{0,4},{1,5},{2,6},{3,7},{4,0},{5,1},{6,2},{7,3},{8,12},{9,13},{10,... | collective-permute-start | bytes 196616 | tf_op jit(solution)/shard_map/ppermute | solution.py:17
  141.6 4.5 %collective-permute-start.35 = (f32[32,512]{1,0:T(8,128)}, f32[32,512]{1,0:T(8,128)S(1)}, u32[]{:S(2)}, u32[]{:S(2)}) collective-permute-start(f32[32,512]{1,0:T(8,128)} %shard_map.97.own), channel_id=1, source_target_pairs={{0,8},{8,0},{16,24},{24,16},{1,9},{9,1},{17,25},{25,17},{2,10},{10... | collective-permute-start | bytes 196616 | tf_op jit(solution)/shard_map/ppermute | solution.py:17
  149.0 4.5 %collective-permute-start.36 = (f32[32,512]{1,0:T(8,128)}, f32[32,512]{1,0:T(8,128)S(1)}, u32[]{:S(2)}, u32[]{:S(2)}) collective-permute-start(f32[32,512]{1,0:T(8,128)} %get-tuple-element.84.own), channel_id=1, source_target_pairs={{0,4},{1,5},{2,6},{3,7},{4,0},{5,1},{6,2},{7,3},{8,12},{9,13},{10,... | collective-permute-start | bytes 196616 | tf_op jit(solution)/shard_map/ppermute | solution.py:17
  149.8 8.0 %collective-permute-start.40 = (f32[2,32,64]{2,1,0:T(8,128)}, f32[2,32,64]{2,1,0:T(8,128)S(1)}, u32[]{:S(2)}, u32[]{:S(2)}) collective-permute-start(f32[2,32,64]{2,1,0:T(8,128)} %get-tuple-element.90), channel_id=1, source_target_pairs={{0,1},{1,0},{2,3},{3,2},{4,5},{5,4},{6,7},{7,6},{8,9},{9,8},{10,11... | collective-permute-start | bytes 49160 | tf_op jit(solution)/shard_map/ppermute | solution.py:17
  149.8 8.3 %collective-permute-start.41 = (f32[2,32,64]{2,1,0:T(8,128)}, f32[2,32,64]{2,1,0:T(8,128)S(1)}, u32[]{:S(2)}, u32[]{:S(2)}) collective-permute-start(f32[2,32,64]{2,1,0:T(8,128)} %get-tuple-element.91), channel_id=1, source_target_pairs={{0,2},{1,3},{2,0},{3,1},{4,6},{5,7},{6,4},{7,5},{8,10},{9,11},{10,... | collective-permute-start | bytes 49160 | tf_op jit(solution)/shard_map/ppermute | solution.py:17
  151.4 6.8 %collective-permute-start.42 = (f32[2,32,64]{2,1,0:T(8,128)}, f32[2,32,64]{2,1,0:T(8,128)S(1)}, u32[]{:S(2)}, u32[]{:S(2)}) collective-permute-start(f32[2,32,64]{2,1,0:T(8,128)} %get-tuple-element.92), channel_id=1, source_target_pairs={{0,3},{1,2},{2,1},{3,0},{4,7},{5,6},{6,5},{7,4},{8,11},{9,10},{10,... | collective-permute-start | bytes 49160 | tf_op jit(solution)/shard_map/ppermute | solution.py:17
  156.3 1.9 %collective-permute-start.37 = (f32[32,64]{1,0:T(8,128)}, f32[32,64]{1,0:T(8,128)S(1)}, u32[]{:S(2)}, u32[]{:S(2)}) collective-permute-start(f32[32,64]{1,0:T(8,128)} %get-tuple-element.86), channel_id=1, source_target_pairs={{0,1},{1,0},{2,3},{3,2},{4,5},{5,4},{6,7},{7,6},{8,9},{9,8},{10,11... | collective-permute-start | bytes 24584 | tf_op jit(solution)/shard_map/ppermute | solution.py:17
  156.3 4.0 %collective-permute-start.38 = (f32[32,64]{1,0:T(8,128)}, f32[32,64]{1,0:T(8,128)S(1)}, u32[]{:S(2)}, u32[]{:S(2)}) collective-permute-start(f32[32,64]{1,0:T(8,128)} %get-tuple-element.87), channel_id=1, source_target_pairs={{0,2},{1,3},{2,0},{3,1},{4,6},{5,7},{6,4},{7,5},{8,10},{9,11},{10,... | collective-permute-start | bytes 24584 | tf_op jit(solution)/shard_map/ppermute | solution.py:17
  157.8 3.4 %collective-permute-start.39 = (f32[32,64]{1,0:T(8,128)}, f32[32,64]{1,0:T(8,128)S(1)}, u32[]{:S(2)}, u32[]{:S(2)}) collective-permute-start(f32[32,64]{1,0:T(8,128)} %get-tuple-element.88), channel_id=1, source_target_pairs={{0,3},{1,2},{2,1},{3,0},{4,7},{5,6},{6,5},{7,4},{8,11},{9,10},{10,... | collective-permute-start | bytes 24584 | tf_op jit(solution)/shard_map/ppermute | solution.py:17
  (41 other events, 146.7 us)
